TPU v7x, 256 devices: a whole 4x4x8 slice. The times are simulated.
256 devices in a mesh: dp: 16 (over y, z_hi), expert: 8 (over x, core), tensor: 2 (over z_lo).
Axes of the slice: x: 4, y: 4, z: 8 (z_hi: 4, z_lo: 2; z = z_hi * 2 + z_lo), core: 2. Of those that a mesh axis runs over, the one named last changes fastest.
Arguments:
- tokens: bfloat16 [2048, 5120], P('dp', 'tensor'), may hold values from -6 to 6
- routes: int32 [2048, 6], P('dp'), may hold values from 0 to 15, all different within a row; in each aligned block of 128 rows (0 to 127, 128 to 255, ...) at most 72 rows name the same one
- route_weights: float32 [2048, 6], P('dp'), may hold values from 0.05 to 0.5
- gate_weight: bfloat16 [16, 1536, 5120], P('dp', 'expert', 'tensor'), may hold values from -0.078125 to 0.078125
- up_weight: bfloat16 [16, 1536, 5120], P('dp', 'expert', 'tensor'), may hold values from -0.078125 to 0.078125
- down_weight: bfloat16 [16, 1536, 5120], P('dp', 'expert', 'tensor'), may hold values from -0.15625 to 0.15625
- cotangent: bfloat16 [2048, 5120], P('dp', 'tensor'), may hold values from -6 to 6
Outputs:
- layer_out: bfloat16 [2048, 5120], P('dp', 'tensor')
- token_grad: bfloat16 [2048, 5120], P('dp', 'tensor')
- gate_grad: float32 [16, 1536, 5120], P('dp', 'expert', 'tensor')
- up_grad: float32 [16, 1536, 5120], P('dp', 'expert', 'tensor')
- down_grad: float32 [16, 1536, 5120], P('dp', 'expert', 'tensor')
Inputs may be any that keep to these rules, and one draw needn't show every extreme that they name: `routes`: each row names 6 different experts. In the rows of one index of dp (aligned blocks of 128 rows) no expert is named by more than 72 rows, a bound that some block reaches.
All inputs are finite; a program needn't handle non-finite values.
Results may differ from a plain program's by a relative error of at most 0.023.
Values may be sent and summed in bfloat16 or wider, within the bound.
A program may use at most 128 MiB of HBM per device.

v0:
```python
import jax
import jax.numpy as jnp
from jax import lax
from jax.sharding import PartitionSpec as P


def body(tokens, routes, route_weights, gate_weight, up_weight, down_weight, cotangent):
    dp_count = lax.axis_size("dp")
    hidden_split = lax.axis_size("expert")
    local_exp, hidden_share, half_width = gate_weight.shape
    tok_rows, top_count = routes.shape
    experts = local_exp * dp_count
    capacity = min(tok_rows, 3 * tok_rows * top_count // (2 * experts))
    share_rows = capacity // hidden_split
    pair_count = tok_rows * top_count
    slot_count = experts * capacity
    flat_route = routes.reshape(pair_count)
    onehot = (flat_route[:, None] == jnp.arange(experts, dtype=jnp.int32)[None, :]).astype(
        jnp.int32
    )
    position = jnp.sum((jnp.cumsum(onehot, axis=0) - 1) * onehot, axis=1)
    target = flat_route * capacity + position
    selector = jnp.arange(slot_count, dtype=jnp.int32)[:, None] == target[None, :]
    place_tok = jnp.any(selector.reshape(slot_count, tok_rows, top_count), axis=2).astype(
        jnp.bfloat16
    )
    flat_weight = route_weights.reshape(pair_count)
    slot_weight = jnp.sum(jnp.where(selector, flat_weight[None, :], jnp.float32(0.0)), axis=1)
    pair_token = jnp.arange(pair_count, dtype=jnp.int32) // top_count
    slot_token = jnp.sum(jnp.where(selector, pair_token[None, :], 0), axis=1)
    slot_used = jnp.any(selector, axis=1)
    slot_token = jnp.where(slot_used, slot_token, tok_rows)
    own_start = lax.axis_index("expert") * share_rows
    own_place = lax.dynamic_slice_in_dim(
        place_tok.reshape(experts, capacity, tok_rows), own_start, share_rows, 1
    )
    own_place = own_place.reshape(experts * share_rows, tok_rows)
    own_weight = lax.dynamic_slice_in_dim(
        slot_weight.reshape(experts, capacity), own_start, share_rows, 1
    )
    own_weight = own_weight.reshape(experts * share_rows)
    own_token = lax.dynamic_slice_in_dim(
        slot_token.reshape(experts, capacity), own_start, share_rows, 1
    )
    own_token = own_token.reshape(experts * share_rows)

    def send_rows(slot_rows):
        slot_grid = slot_rows.reshape(dp_count, local_exp, capacity, half_width)
        arrived = lax.all_to_all(slot_grid, "dp", split_axis=0, concat_axis=2, tiled=True)
        return arrived.reshape(local_exp, dp_count, capacity, half_width)

    def width_sum(partial_values):
        return lax.psum(partial_values.astype(jnp.bfloat16), "tensor").astype(jnp.float32)

    def reduce_rows(partial_rows):
        slot_grid = partial_rows.reshape(local_exp, dp_count, capacity, half_width)
        summed = lax.psum_scatter(
            slot_grid.astype(jnp.bfloat16), "expert", scatter_dimension=2, tiled=True
        )
        return summed

    def send_home(share_block):
        returned = lax.all_to_all(share_block, "dp", split_axis=1, concat_axis=0, tiled=True)
        return returned.reshape(experts * share_rows, half_width)

    def token_sum(partial_tokens):
        return lax.psum(partial_tokens.astype(jnp.bfloat16), "expert").astype(jnp.float32)

    token_slots = jnp.dot(place_tok, tokens, preferred_element_type=jnp.float32).astype(
        jnp.bfloat16
    )
    rows = send_rows(token_slots)
    flat_rows = rows.reshape(local_exp, dp_count * capacity, half_width)
    gate_part = jnp.einsum(
        "lrd,lfd->lrf", flat_rows, gate_weight, preferred_element_type=jnp.float32
    )
    up_part = jnp.einsum("lrd,lfd->lrf", flat_rows, up_weight, preferred_element_type=jnp.float32)
    both_values = width_sum(jnp.stack((gate_part, up_part)))
    gate_val = both_values[0]
    up_val = both_values[1]
    sigmoid_gate = jax.nn.sigmoid(gate_val)
    activated = gate_val * sigmoid_gate
    hidden = (activated * up_val).astype(jnp.bfloat16)
    down_part = jnp.einsum("lrf,lfd->lrd", hidden, down_weight, preferred_element_type=jnp.float32)
    expert_out = send_home(reduce_rows(down_part))
    weighted = own_weight[:, None] * expert_out.astype(jnp.float32)
    out_part = (
        jnp.zeros((tok_rows, half_width), jnp.float32).at[own_token].add(weighted, mode="drop")
    )
    layer_out = token_sum(out_part).astype(jnp.bfloat16)
    pair_grad = (
        flat_weight[:, None] * jnp.repeat(cotangent, top_count, axis=0).astype(jnp.float32)
    ).astype(jnp.bfloat16)
    grad_slots = jnp.dot(
        selector.astype(jnp.bfloat16), pair_grad, preferred_element_type=jnp.float32
    ).astype(jnp.bfloat16)
    grad_rows = send_rows(grad_slots).reshape(local_exp, dp_count * capacity, half_width)
    hidden_grad = width_sum(
        jnp.einsum("lrd,lfd->lrf", grad_rows, down_weight, preferred_element_type=jnp.float32)
    )
    gate_delta = (
        hidden_grad * up_val * sigmoid_gate * (1.0 + gate_val * (1.0 - sigmoid_gate))
    ).astype(jnp.bfloat16)
    up_delta = (hidden_grad * activated).astype(jnp.bfloat16)
    input_part = jnp.einsum(
        "lrf,lfd->lrd", gate_delta, gate_weight, preferred_element_type=jnp.float32
    )
    input_part = input_part + jnp.einsum(
        "lrf,lfd->lrd", up_delta, up_weight, preferred_element_type=jnp.float32
    )
    row_grad = send_home(reduce_rows(input_part))
    grad_part = jnp.einsum("st,sd->td", own_place, row_grad, preferred_element_type=jnp.float32)
    token_grad = token_sum(grad_part).astype(jnp.bfloat16)
    gate_grad = jnp.einsum(
        "lrf,lrd->lfd", gate_delta, flat_rows, preferred_element_type=jnp.float32
    )
    up_grad = jnp.einsum("lrf,lrd->lfd", up_delta, flat_rows, preferred_element_type=jnp.float32)
    down_grad = jnp.einsum("lrf,lrd->lfd", hidden, grad_rows, preferred_element_type=jnp.float32)
    return (layer_out, token_grad, gate_grad, up_grad, down_grad)


def solution(mesh):
    in_specs = (
        P("dp", "tensor"),
        P("dp", None),
        P("dp", None),
        P("dp", "expert", "tensor"),
        P("dp", "expert", "tensor"),
        P("dp", "expert", "tensor"),
        P("dp", "tensor"),
    )
    out_specs = (
        P("dp", "tensor"),
        P("dp", "tensor"),
        P("dp", "expert", "tensor"),
        P("dp", "expert", "tensor"),
        P("dp", "expert", "tensor"),
    )
    return jax.shard_map(body, mesh=mesh, in_specs=in_specs, out_specs=out_specs, check_vma=False)
```

profile of v0, /device:TPU:8, one launch (start us, length us, event | category | flops | bytes accessed | tf_op | source)
XLA Modules:
  0.0 626.3 jit_solution(9417354293102109201)
XLA Ops:
  12.0 5.4 convolution_convert_fusion.1
  17.3 11.7 %all-to-all-start = ((bf16[16,1,72,2560]{3,2,1,0:T(8,128)(2,1)}), bf16[16,1,72,2560]{3,2,1,0:T(8,128)(2,1)}, u32[]{:S(2)}, u32[]{:S(2)}) async-start(bf16[16,1,72,2560]{3,2,1,0:T(8,128)(2,1)} %bitcast.114), calls=%async_computation | async-start | bytes 11796480 | tf_op jit(solution)/shard_map/all_to_all | solution.py:49
  29.3 5.3 broadcast_in_dim.48
  34.6 9.5 %convert_element_type.111 = f32[768,2560]{1,0:T(8,128)} reshape(f32[128,6,2560]{2,1,0:T(8,128)} %broadcast_in_dim.48) | data formatting | bytes 15728640 | tf_op jit(solution)/shard_map/convert_element_type | solution.py:92
  44.1 9.9 %convolution_convert_fusion = bf16[1152,2560]{1,0:T(8,128)(2,1)} fusion(f32[768,2560]{1,0:T(8,128)} %convert_element_type.111, f32[768]{0:T(1024)S(1)} %broadcast_in_dim.45, s32[768]{0:T(1024)S(1)} %get-tuple-element.10), kind=kOutput, calls=%fused_computation.2 | convolution fusion | flops 4537614336 | bytes 13768704 | tf_op jit(solution)/shard_map/dot_general | solution.py:94
  54.0 108.3 %all-to-all-done = bf16[16,1,72,2560]{3,2,1,0:T(8,128)(2,1)} async-done(((bf16[16,1,72,2560]{3,2,1,0:T(8,128)(2,1)}), bf16[16,1,72,2560]{3,2,1,0:T(8,128)(2,1)}, u32[]{:S(2)}, u32[]{:S(2)}) %all-to-all-start) | async-done | bytes 5898272 | tf_op jit(solution)/shard_map/all_to_all | solution.py:49
  162.3 6.2 all-to-all-start.2
  168.6 5.1 fusion.6
  173.7 4.7 fusion.5
  179.4 103.4 %all-to-all-done.2 = bf16[16,1,72,2560]{3,2,1,0:T(8,128)(2,1)} async-done(((bf16[16,1,72,2560]{3,2,1,0:T(8,128)(2,1)}), bf16[16,1,72,2560]{3,2,1,0:T(8,128)(2,1)}, u32[]{:S(2)}, u32[]{:S(2)}) %all-to-all-start.2) | async-done | bytes 5898272 | tf_op jit(solution)/shard_map/all_to_all | solution.py:49
  282.9 5.5 fusion.7
  288.6 112.7 %all-reduce.7.cloned.1.call-done = (bf16[2,1,1152,192]{2,3,1,0:T(8,128)(2,1)}, bf16[1,1152,192]{1,2,0:T(8,128)(2,1)}) async-done(((bf16[2,1,1152,192]{2,3,1,0:T(8,128)(2,1)}, bf16[1,1152,192]{1,2,0:T(8,128)(2,1)}), (bf16[2,1,1152,192]{2,3,1,0:T(8,128)(2,1)}, bf16[1,1152,192]{1,2,0:T(8,128)(2,1)})) %all-reduce.7.cloned.1.call-update) | async-done | bytes 1327120 | tf_op jit(solution)/shard_map/psum | solution.py:53
  406.7 4.3 copy.55
  417.3 4.4 copy.58
  421.7 33.9 %reduce-scatter.3.cloned.1.call-done = bf16[1,16,9,2560]{3,1,0,2:T(8,128)(2,1)} async-done(((bf16[1,16,72,2560]{3,1,0,2:T(8,128)(2,1)}), bf16[1,16,9,2560]{3,1,0,2:T(8,128)(2,1)}) %reduce-scatter.3.cloned.1.call-update) | async-done | bytes 737296 | tf_op jit(solution)/shard_map/reduce_scatter | solution.py:57
  458.2 10.0 %all-to-all-start.1 = ((bf16[1,16,9,2560]{3,2,0,1:T(8,128)(2,1)}), bf16[1,16,9,2560]{3,2,0,1:T(8,128)(2,1)}, u32[]{:S(2)}, u32[]{:S(2)}) async-start(bf16[1,16,9,2560]{3,2,0,1:T(8,128)(2,1)} %copy.56), calls=%async_computation.2 | async-start | bytes 2621440 | tf_op jit(solution)/shard_map/all_to_all | solution.py:63
  469.1 33.4 %reduce-scatter.5.cloned.1.call-done = bf16[1,16,9,2560]{3,1,0,2:T(8,128)(2,1)} async-done(((bf16[1,16,72,2560]{3,1,0,2:T(8,128)(2,1)}), bf16[1,16,9,2560]{3,1,0,2:T(8,128)(2,1)}) %reduce-scatter.5.cloned.1.call-update) | async-done | bytes 737296 | tf_op jit(solution)/shard_map/reduce_scatter | solution.py:57
  505.1 10.0 %all-to-all-start.3 = ((bf16[1,16,9,2560]{3,2,0,1:T(8,128)(2,1)}), bf16[1,16,9,2560]{3,2,0,1:T(8,128)(2,1)}, u32[]{:S(2)}, u32[]{:S(2)}) async-start(bf16[1,16,9,2560]{3,2,0,1:T(8,128)(2,1)} %copy.59), calls=%async_computation.5 | async-start | bytes 2621440 | tf_op jit(solution)/shard_map/all_to_all | solution.py:63
  517.0 5.4 convolution_bitcast_fusion
  525.1 4.7 scatter_custom_fusion
  532.1 14.4 %all-to-all-done.3 = bf16[1,16,9,2560]{3,2,0,1:T(8,128)(2,1)} async-done(((bf16[1,16,9,2560]{3,2,0,1:T(8,128)(2,1)}), bf16[1,16,9,2560]{3,2,0,1:T(8,128)(2,1)}, u32[]{:S(2)}, u32[]{:S(2)}) %all-to-all-start.3) | async-done | bytes 737312 | tf_op jit(solution)/shard_map/all_to_all | solution.py:63
  549.4 5.4 convolution_bitcast_fusion.2
  554.8 5.5 convolution_bitcast_fusion.1
  560.3 55.5 %all-reduce.5.cloned.1.call-done = (bf16[128,2560]{1,0:T(8,128)(2,1)}, bf16[128,2560]{1,0:T(8,128)(2,1)}) async-done(((bf16[128,2560]{1,0:T(8,128)(2,1)}, bf16[128,2560]{1,0:T(8,128)(2,1)}), (bf16[128,2560]{1,0:T(8,128)(2,1)}, bf16[128,2560]{1,0:T(8,128)(2,1)})) %all-reduce.5.cloned.1.call-update) | async-done | bytes 1310736 | tf_op jit(solution)/shard_map/psum | solution.py:67
  (71 shorter events, 37.6 us)
Async XLA Ops:
  7.2 275.7 %copy-start = (bf16[1,192,2560]{2,1,0:T(8,128)(2,1)S(1)}, bf16[1,192,2560]{2,1,0:T(8,128)(2,1)}, u32[]{:S(2)}) copy-start(bf16[1,192,2560]{2,1,0:T(8,128)(2,1)} %param.12) | copy-start | bytes 2949124
  12.0 5.4 copy-start.4
  17.3 11.7 %copy-start.8 = (f32[128,6]{0,1:T(8,128)S(1)}, f32[128,6]{0,1:T(8,128)}, u32[]{:S(2)}) copy-start(f32[128,6]{0,1:T(8,128)} %param.9) | copy-start | bytes 9220
  17.3 12.0 %copy-start.7 = (bf16[128,2560]{1,0:T(8,128)(2,1)S(1)}, bf16[128,2560]{1,0:T(8,128)(2,1)}, u32[]{:S(2)}) copy-start(bf16[128,2560]{1,0:T(8,128)(2,1)} %param.13) | copy-start | bytes 1966084
  17.3 144.9 %all-to-all-start = ((bf16[16,1,72,2560]{3,2,1,0:T(8,128)(2,1)}), bf16[16,1,72,2560]{3,2,1,0:T(8,128)(2,1)}, u32[]{:S(2)}, u32[]{:S(2)}) async-start(bf16[16,1,72,2560]{3,2,1,0:T(8,128)(2,1)} %bitcast.114), calls=%async_computation | async-start | bytes 11796480 | tf_op jit(solution)/shard_map/all_to_all | solution.py:49
  162.3 120.6 %all-to-all-start.2 = ((bf16[16,1,72,2560]{3,2,1,0:T(8,128)(2,1)}), bf16[16,1,72,2560]{3,2,1,0:T(8,128)(2,1)}, u32[]{:S(2)}, u32[]{:S(2)}) async-start(bf16[16,1,72,2560]{3,2,1,0:T(8,128)(2,1)} %bitcast.116), calls=%async_computation.3 | async-start | bytes 11796480 | tf_op jit(solution)/shard_map/all_to_all | solution.py:49
  168.5 232.8 %all-reduce.7.cloned.1.call-start = ((), (), s32[]{:S(2)}) async-start(), calls=%async_computation.9 | async-start | bytes 2654208 | tf_op jit(solution)/shard_map/psum | solution.py:53
  168.6 5.1 copy-start.5
  288.4 167.2 %reduce-scatter.3.cloned.1.call-start = ((), (), s32[]{:S(2)}) async-start(), calls=%async_computation.6 | async-start | bytes 6635520 | tf_op jit(solution)/shard_map/reduce_scatter | solution.py:57
  411.0 1.0 copy-start.2
  411.0 91.5 %reduce-scatter.5.cloned.1.call-start = ((), (), s32[]{:S(2)}) async-start(), calls=%async_computation.7 | async-start | bytes 6635520 | tf_op jit(solution)/shard_map/reduce_scatter | solution.py:57
  412.4 3.0 copy-start.6
  458.2 46.9 %all-to-all-start.1 = ((bf16[1,16,9,2560]{3,2,0,1:T(8,128)(2,1)}), bf16[1,16,9,2560]{3,2,0,1:T(8,128)(2,1)}, u32[]{:S(2)}, u32[]{:S(2)}) async-start(bf16[1,16,9,2560]{3,2,0,1:T(8,128)(2,1)} %copy.56), calls=%async_computation.2 | async-start | bytes 2621440 | tf_op jit(solution)/shard_map/all_to_all | solution.py:63
  505.1 41.4 %all-to-all-start.3 = ((bf16[1,16,9,2560]{3,2,0,1:T(8,128)(2,1)}), bf16[1,16,9,2560]{3,2,0,1:T(8,128)(2,1)}, u32[]{:S(2)}, u32[]{:S(2)}) async-start(bf16[1,16,9,2560]{3,2,0,1:T(8,128)(2,1)} %copy.59), calls=%async_computation.5 | async-start | bytes 2621440 | tf_op jit(solution)/shard_map/all_to_all | solution.py:63
  515.1 100.7 %all-reduce.5.cloned.1.call-start = ((), (), s32[]{:S(2)}) async-start(), calls=%async_computation.8 | async-start | bytes 2621440 | tf_op jit(solution)/shard_map/psum | solution.py:67
  549.4 5.4 copy-start.3
  554.8 65.0 %copy-start.1 = (bf16[1,192,2560]{2,1,0:T(8,128)(2,1)S(1)}, bf16[1,192,2560]{2,1,0:T(8,128)(2,1)}, u32[]{:S(2)}) copy-start(bf16[1,192,2560]{2,1,0:T(8,128)(2,1)} %param.12) | copy-start | bytes 2949124
Sparse Core Ops, SparseCore 0:
  288.5 112.7 all-reduce.6
  411.2 44.3 reduce-scatter.2
  458.1 44.3 reduce-scatter.4
  549.5 66.3 all-reduce.4
where the time goes:
time: 628 us; the launch traced here: 626 us
  waiting for transfers between devices  462 us (74%)
  matrix products  55.8 us (9%)
  local copies, waits for them, and re-layouts  42.2 us (7%)
  starting transfers between devices  38.3 us (6%)
  other arithmetic  14.3 us (2%)
  between operations  14 us (2%)
    all_to_all x2, waiting for transfers between devices, send_rows(): lax.all_to_all(slot_grid, 'dp', split_axis=0, concat_axis=2, tiled=True)  212 us
    psum x1, waiting for transfers between devices, width_sum(): lax.psum(partial_values.astype(jnp.bfloat16), 'tensor').astype(jnp.float32)  113 us
    reduce_scatter x2, waiting for transfers between devices, reduce_rows(): lax.psum_scatter(slot_grid.astype(jnp.bfloat16), 'expert', scatter_dimens...  67.3 us
    psum x1, waiting for transfers between devices, token_sum(): lax.psum(partial_tokens.astype(jnp.bfloat16), 'expert').astype(jnp.float32)  55.5 us
    all_to_all x2, starting transfers between devices, send_home(): lax.all_to_all(share_block, 'dp', split_axis=1, concat_axis=0, tiled=True)  20 us
    all_to_all x2, starting transfers between devices, send_rows(): lax.all_to_all(slot_grid, 'dp', split_axis=0, concat_axis=2, tiled=True)  17.9 us
    all_to_all x2, waiting for transfers between devices, send_home(): lax.all_to_all(share_block, 'dp', split_axis=1, concat_axis=0, tiled=True)  14.4 us
  transfers between devices with their start and end apart: 8, of which 7 were waited for; matrix products, arithmetic and copies ran while one was open for 13% of the time, Pallas kernels for 0%

commit v1 on v0

--- a/solution.py
+++ b/solution.py
@@ -2,6 +2,11 @@
 import jax.numpy as jnp
 from jax import lax
 from jax.sharding import PartitionSpec as P
+
+
+def gather_and_add(value, name):
+    terms = lax.all_gather(value, name)
+    return jnp.sum(terms, axis=0)
 
 
 def body(tokens, routes, route_weights, gate_weight, up_weight, down_weight, cotangent):
@@ -50,7 +55,7 @@
         return arrived.reshape(local_exp, dp_count, capacity, half_width)
 
     def width_sum(partial_values):
-        return lax.psum(partial_values.astype(jnp.bfloat16), "tensor").astype(jnp.float32)
+        return gather_and_add(partial_values.astype(jnp.bfloat16), "tensor").astype(jnp.float32)
 
     def reduce_rows(partial_rows):
         slot_grid = partial_rows.reshape(local_exp, dp_count, capacity, half_width)

time: 628 us -> 582 us (0.927)
  waiting for transfers between devices: 462 us -> 376 us
  blocking collectives: 0 us -> 33.6 us
  other arithmetic: 14.3 us -> 22 us
    psum x1 -> x0, waiting for transfers between devices: 113 us -> none  [width_sum(): lax.psum(partial_values.astype(jnp.bfloat16), 'tensor').astype(jnp.float32)]
    all_gather x0 -> x1, blocking collectives: none -> 33.6 us  [gather_and_add(): terms = lax.all_gather(value, name)]
    all_to_all x2, waiting for transfers between devices: 212 us -> 242 us  [send_rows(): lax.all_to_all(slot_grid, 'dp', split_axis=0, concat_axis=2, tiled=True)]
  transfers between devices with their start and end apart: 8 -> 8, of which waited for: 7 -> 6; matrix products, arithmetic and copies ran while one was open for 13% -> 15% of each run, Pallas kernels for 0% -> 0%
where the time goes in v1:
time: 582 us; the launch traced here: 581 us
  waiting for transfers between devices  376 us (65%)
  matrix products  54.7 us (9%)
  local copies, waits for them, and re-layouts  42.5 us (7%)
  starting transfers between devices  38.5 us (7%)
  blocking collectives  33.6 us (6%)
  other arithmetic  22 us (4%)
  between operations  14 us (2%)
    all_to_all x2, waiting for transfers between devices, send_rows(): lax.all_to_all(slot_grid, 'dp', split_axis=0, concat_axis=2, tiled=True)  242 us
    reduce_scatter x2, waiting for transfers between devices, reduce_rows(): lax.psum_scatter(slot_grid.astype(jnp.bfloat16), 'expert', scatter_dimens...  63.1 us
    psum x1, waiting for transfers between devices, token_sum(): lax.psum(partial_tokens.astype(jnp.bfloat16), 'expert').astype(jnp.float32)  55.5 us
    all_gather x1, blocking collectives, gather_and_add(): terms = lax.all_gather(value, name)  33.6 us
    all_to_all x2, starting transfers between devices, send_home(): lax.all_to_all(share_block, 'dp', split_axis=1, concat_axis=0, tiled=True)  20 us
    all_to_all x2, starting transfers between devices, send_rows(): lax.all_to_all(slot_grid, 'dp', split_axis=0, concat_axis=2, tiled=True)  18.1 us
    all_to_all x2, waiting for transfers between devices, send_home(): lax.all_to_all(share_block, 'dp', split_axis=1, concat_axis=0, tiled=True)  14.6 us
  transfers between devices with their start and end apart: 8, of which 6 were waited for; matrix products, arithmetic and copies ran while one was open for 15% of the time, Pallas kernels for 0%

profile of v1, /device:TPU:8, one launch (start us, length us, event | category | flops | bytes accessed | tf_op | source)
XLA Modules:
  0.0 580.9 jit_solution(12378762998732764299)
XLA Ops:
  12.0 5.4 convolution_convert_fusion.1
  17.3 11.7 %all-to-all-start = ((bf16[16,1,72,2560]{3,2,1,0:T(8,128)(2,1)}), bf16[16,1,72,2560]{3,2,1,0:T(8,128)(2,1)}, u32[]{:S(2)}, u32[]{:S(2)}) async-start(bf16[16,1,72,2560]{3,2,1,0:T(8,128)(2,1)} %bitcast.109), calls=%async_computation | async-start | bytes 11796480 | tf_op jit(solution)/shard_map/all_to_all | solution.py:54
  29.3 5.3 broadcast_in_dim.48
  34.6 9.5 %convert_element_type.169 = f32[768,2560]{1,0:T(8,128)} reshape(f32[128,6,2560]{2,1,0:T(8,128)} %broadcast_in_dim.48) | data formatting | bytes 15728640 | tf_op jit(solution)/shard_map/convert_element_type | solution.py:97
  44.1 9.9 %convolution_convert_fusion = bf16[1152,2560]{1,0:T(8,128)(2,1)} fusion(f32[768,2560]{1,0:T(8,128)} %convert_element_type.169, f32[768]{0:T(1024)S(1)} %broadcast_in_dim.45, s32[768]{0:T(1024)S(1)} %get-tuple-element.10), kind=kOutput, calls=%fused_computation.2 | convolution fusion | flops 4537614336 | bytes 13768704 | tf_op jit(solution)/shard_map/dot_general | solution.py:99
  54.0 108.3 %all-to-all-done = bf16[16,1,72,2560]{3,2,1,0:T(8,128)(2,1)} async-done(((bf16[16,1,72,2560]{3,2,1,0:T(8,128)(2,1)}), bf16[16,1,72,2560]{3,2,1,0:T(8,128)(2,1)}, u32[]{:S(2)}, u32[]{:S(2)}) %all-to-all-start) | async-done | bytes 5898272 | tf_op jit(solution)/shard_map/all_to_all | solution.py:54
  162.3 6.4 %all-to-all-start.2 = ((bf16[16,1,72,2560]{3,2,1,0:T(8,128)(2,1)}), bf16[16,1,72,2560]{3,2,1,0:T(8,128)(2,1)}, u32[]{:S(2)}, u32[]{:S(2)}) async-start(bf16[16,1,72,2560]{3,2,1,0:T(8,128)(2,1)} %bitcast.111), calls=%async_computation.3 | async-start | bytes 11796480 | tf_op jit(solution)/shard_map/all_to_all | solution.py:54
  168.7 4.8 fusion.6
  173.6 4.7 fusion.5
  179.4 134.0 %all-to-all-done.2 = bf16[16,1,72,2560]{3,2,1,0:T(8,128)(2,1)} async-done(((bf16[16,1,72,2560]{3,2,1,0:T(8,128)(2,1)}), bf16[16,1,72,2560]{3,2,1,0:T(8,128)(2,1)}, u32[]{:S(2)}, u32[]{:S(2)}) %all-to-all-start.2) | async-done | bytes 5898272 | tf_op jit(solution)/shard_map/all_to_all | solution.py:54
  313.3 4.7 convolution_convert_fusion.4
  318.1 33.6 %all-gather = bf16[2304,192]{0,1:T(8,128)(2,1)S(1)} all-gather(bf16[1152,192]{0,1:T(8,128)(2,1)S(1)} %convolution_convert_fusion.4), channel_id=2, replica_groups=mesh['dp'=16,'expert'=8,'tensor'=2] {'tensor'}, dimensions={0}, use_global_device_ids=true | all-gather | bytes 1327104 | tf_op jit(solution)/shard_map/all_gather | solution.py:8
  366.3 4.3 copy.66
  375.8 4.4 copy.69
  380.2 29.7 %reduce-scatter.3.cloned.1.call-done = bf16[1,16,9,2560]{3,1,0,2:T(8,128)(2,1)} async-done(((bf16[1,16,72,2560]{3,1,0,2:T(8,128)(2,1)}), bf16[1,16,9,2560]{3,1,0,2:T(8,128)(2,1)}) %reduce-scatter.3.cloned.1.call-update) | async-done | bytes 737296 | tf_op jit(solution)/shard_map/reduce_scatter | solution.py:62
  412.5 10.2 %all-to-all-start.1 = ((bf16[1,16,9,2560]{3,2,0,1:T(8,128)(2,1)}), bf16[1,16,9,2560]{3,2,0,1:T(8,128)(2,1)}, u32[]{:S(2)}, u32[]{:S(2)}) async-start(bf16[1,16,9,2560]{3,2,0,1:T(8,128)(2,1)} %copy.67), calls=%async_computation.2 | async-start | bytes 2621440 | tf_op jit(solution)/shard_map/all_to_all | solution.py:68
  423.6 33.4 %reduce-scatter.5.cloned.1.call-done = bf16[1,16,9,2560]{3,1,0,2:T(8,128)(2,1)} async-done(((bf16[1,16,72,2560]{3,1,0,2:T(8,128)(2,1)}), bf16[1,16,9,2560]{3,1,0,2:T(8,128)(2,1)}) %reduce-scatter.5.cloned.1.call-update) | async-done | bytes 737296 | tf_op jit(solution)/shard_map/reduce_scatter | solution.py:62
  459.7 9.9 %all-to-all-start.3 = ((bf16[1,16,9,2560]{3,2,0,1:T(8,128)(2,1)}), bf16[1,16,9,2560]{3,2,0,1:T(8,128)(2,1)}, u32[]{:S(2)}, u32[]{:S(2)}) async-start(bf16[1,16,9,2560]{3,2,0,1:T(8,128)(2,1)} %copy.70), calls=%async_computation.5 | async-start | bytes 2621440 | tf_op jit(solution)/shard_map/all_to_all | solution.py:68
  471.5 5.4 convolution_bitcast_fusion
  479.6 4.7 scatter_custom_fusion
  486.5 14.6 %all-to-all-done.3 = bf16[1,16,9,2560]{3,2,0,1:T(8,128)(2,1)} async-done(((bf16[1,16,9,2560]{3,2,0,1:T(8,128)(2,1)}), bf16[1,16,9,2560]{3,2,0,1:T(8,128)(2,1)}, u32[]{:S(2)}, u32[]{:S(2)}) %all-to-all-start.3) | async-done | bytes 737312 | tf_op jit(solution)/shard_map/all_to_all | solution.py:68
  504.0 5.4 convolution_bitcast_fusion.2
  509.4 5.5 convolution_bitcast_fusion.1
  514.9 55.5 %all-reduce.3.cloned.1.call-done = (bf16[128,2560]{1,0:T(8,128)(2,1)}, bf16[128,2560]{1,0:T(8,128)(2,1)}) async-done(((bf16[128,2560]{1,0:T(8,128)(2,1)}, bf16[128,2560]{1,0:T(8,128)(2,1)}), (bf16[128,2560]{1,0:T(8,128)(2,1)}, bf16[128,2560]{1,0:T(8,128)(2,1)})) %all-reduce.3.cloned.1.call-update) | async-done | bytes 1310736 | tf_op jit(solution)/shard_map/psum | solution.py:72
  (78 shorter events, 45.7 us)
Async XLA Ops:
  7.2 306.2 %copy-start = (bf16[1,192,2560]{2,1,0:T(8,128)(2,1)S(1)}, bf16[1,192,2560]{2,1,0:T(8,128)(2,1)}, u32[]{:S(2)}) copy-start(bf16[1,192,2560]{2,1,0:T(8,128)(2,1)} %param.12) | copy-start | bytes 2949124
  12.0 5.4 copy-start.5
  17.3 11.7 %copy-start.10 = (f32[128,6]{0,1:T(8,128)S(1)}, f32[128,6]{0,1:T(8,128)}, u32[]{:S(2)}) copy-start(f32[128,6]{0,1:T(8,128)} %param.9) | copy-start | bytes 9220
  17.3 12.0 %copy-start.9 = (bf16[128,2560]{1,0:T(8,128)(2,1)S(1)}, bf16[128,2560]{1,0:T(8,128)(2,1)}, u32[]{:S(2)}) copy-start(bf16[128,2560]{1,0:T(8,128)(2,1)} %param.13) | copy-start | bytes 1966084
  17.3 144.9 %all-to-all-start = ((bf16[16,1,72,2560]{3,2,1,0:T(8,128)(2,1)}), bf16[16,1,72,2560]{3,2,1,0:T(8,128)(2,1)}, u32[]{:S(2)}, u32[]{:S(2)}) async-start(bf16[16,1,72,2560]{3,2,1,0:T(8,128)(2,1)} %bitcast.109), calls=%async_computation | async-start | bytes 11796480 | tf_op jit(solution)/shard_map/all_to_all | solution.py:54
  162.3 6.4 %copy-start.7 = (bf16[1,192,2560]{2,1,0:T(8,128)(2,1)S(1)}, bf16[1,192,2560]{2,1,0:T(8,128)(2,1)}, u32[]{:S(2)}) copy-start(bf16[1,192,2560]{2,1,0:T(8,128)(2,1)} %param.11) | copy-start | bytes 2949124
  162.3 151.1 %all-to-all-start.2 = ((bf16[16,1,72,2560]{3,2,1,0:T(8,128)(2,1)}), bf16[16,1,72,2560]{3,2,1,0:T(8,128)(2,1)}, u32[]{:S(2)}, u32[]{:S(2)}) async-start(bf16[16,1,72,2560]{3,2,1,0:T(8,128)(2,1)} %bitcast.111), calls=%async_computation.3 | async-start | bytes 11796480 | tf_op jit(solution)/shard_map/all_to_all | solution.py:54
  168.7 186.4 %all-gather.3.cloned.1.call-start = ((), (), s32[]{:S(2)}) async-start(), calls=%async_computation.6 | async-start | bytes 2654208 | tf_op jit(solution)/shard_map/all_gather | solution.py:8
  168.7 4.8 copy-start.6
  179.3 230.6 %reduce-scatter.3.cloned.1.call-start = ((), (), s32[]{:S(2)}) async-start(), calls=%async_computation.7 | async-start | bytes 6635520 | tf_op jit(solution)/shard_map/reduce_scatter | solution.py:62
  370.6 86.4 %reduce-scatter.5.cloned.1.call-start = ((), (), s32[]{:S(2)}) async-start(), calls=%async_computation.8 | async-start | bytes 6635520 | tf_op jit(solution)/shard_map/reduce_scatter | solution.py:62
  370.9 3.1 copy-start.3
  370.9 3.1 copy-start.8
  412.5 58.9 %copy-start.2 = (bf16[1,1,1152,192]{2,3,1,0:T(8,128)(2,1)S(1)}, bf16[1,1,1152,192]{2,3,1,0:T(8,128)(2,1)}, u32[]{:S(2)}) copy-start(bf16[1,1,1152,192]{2,3,1,0:T(8,128)(2,1)} %get-tuple-element.8) | copy-start | bytes 1327108
  412.5 47.2 %all-to-all-start.1 = ((bf16[1,16,9,2560]{3,2,0,1:T(8,128)(2,1)}), bf16[1,16,9,2560]{3,2,0,1:T(8,128)(2,1)}, u32[]{:S(2)}, u32[]{:S(2)}) async-start(bf16[1,16,9,2560]{3,2,0,1:T(8,128)(2,1)} %copy.67), calls=%async_computation.2 | async-start | bytes 2621440 | tf_op jit(solution)/shard_map/all_to_all | solution.py:68
  459.7 41.4 %all-to-all-start.3 = ((bf16[1,16,9,2560]{3,2,0,1:T(8,128)(2,1)}), bf16[1,16,9,2560]{3,2,0,1:T(8,128)(2,1)}, u32[]{:S(2)}, u32[]{:S(2)}) async-start(bf16[1,16,9,2560]{3,2,0,1:T(8,128)(2,1)} %copy.70), calls=%async_computation.5 | async-start | bytes 2621440 | tf_op jit(solution)/shard_map/all_to_all | solution.py:68
  469.6 100.9 %all-reduce.3.cloned.1.call-start = ((), (), s32[]{:S(2)}) async-start(), calls=%async_computation.9 | async-start | bytes 2621440 | tf_op jit(solution)/shard_map/psum | solution.py:72
  504.0 5.4 copy-start.4
  509.4 65.0 %copy-start.1 = (bf16[1,192,2560]{2,1,0:T(8,128)(2,1)S(1)}, bf16[1,192,2560]{2,1,0:T(8,128)(2,1)}, u32[]{:S(2)}) copy-start(bf16[1,192,2560]{2,1,0:T(8,128)(2,1)} %param.12) | copy-start | bytes 2949124
Sparse Core Ops, SparseCore 0:
  179.4 123.7 all-gather.2
  370.7 39.1 reduce-scatter.2
  412.7 44.3 reduce-scatter.4
  504.1 66.3 all-reduce.2
